TPU v7x, 32 devices: a whole 2x2x4 slice. The times are simulated.
32 devices in a mesh: dom: 32 (over z, y, x, core).
Axes of the slice: x: 2, y: 2, z: 4, core: 2. Of those that a mesh axis runs over, the one named last changes fastest.
Arguments:
- positions: float32 [3, 131072], P(None, 'dom'), may hold values from -1.5 to 1.5
- velocity: float32 [3, 131072], P(None, 'dom'), may hold values from -6 to 6
- density_weight: float32 [131072], P('dom'), may hold values from 0.5 to 2
- embed_strength: float32 [131072], P('dom'), may hold values from 0.5 to 2
- occupied: int32 [131072], P('dom'), may hold values 0 or 1
- send_list: int32 [32, 8, 8], P('dom'), may hold values from 0 to 31, as said below
- send_count: int32 [32, 8], P('dom'), may hold values from 0 to 8, as said below
- pair_tiles: int32 [1024, 24], P('dom'), may hold values from 0 to 95, as said below
- pair_count: int32 [1024], P('dom'), may hold values from 1 to 24, as said below
- migrate_dest: int32 [1024], P('dom'), may hold values from 0 to 31, as said below
Outputs:
- force: float32 [3, 131072], P(None, 'dom')
- energy: float32 [131072], P('dom')
- moved: float32 [7, 262144], P(None, 'dom')
- moved_count: int32 [32], P('dom')
Inputs may be any that keep to these rules, and one draw needn't show every extreme that they name: `send_list`: for one domain and one offset the entries are distinct local tile indices. send_count[s, k] counts the tiles domain s sends to domain s - o_k; it is 0 where that domain does not exist and 8 for some pairs. `pair_tiles`: entries index the frame of the tile's domain; a tile's entries are distinct and its first entry is its own local index. `pair_count`: the first tile of every domain uses all 24 slots. `migrate_dest`: A tile's new domain is within 4 of its domain; at most 4 tiles go from one domain to any other, at most 64 tiles to one domain, and both bounds are reached in every draw.
All inputs are finite; a program needn't handle non-finite values. No bound on the sum of `occupied` on one device may be relied on, other than what follows from the above.
Results may differ from a plain program's by a relative error of at most 0.0003.
Values sent between devices are 32-bit elements; how exact they have to be, the bound alone decides.
A program may use at most 64 MiB of HBM per device.

v0:
```python
import math

import jax
import jax.numpy as jnp
from jax import lax
from jax.sharding import PartitionSpec as P

TILE = 128
RADIUS = 4
MMAX = 4


CUTOFF_SQUARE = 4.0
REPULSE = 0.05
TIME_STEP = 0.05
EXACT_PRODUCT = lax.Precision.HIGHEST


def shifted(block, axis, distance):
    devices = range(lax.axis_size(axis))
    route = [(i - distance, i) for i in devices if i - distance in devices]
    return lax.ppermute(block, axis, route)


def prefix(value, axis, combine, identity):
    size, index = (lax.axis_size(axis), lax.axis_index(axis))
    everything = lax.all_gather(value, axis)
    start = jnp.broadcast_to(jnp.asarray(identity, value.dtype), value.shape)

    def step(k, before):
        reached = k < index
        new = combine(before, everything[k])
        return jnp.where(reached, new, before)

    return lax.fori_loop(0, size, step, start)


def offset_list():
    return [position - RADIUS for position in range(RADIUS)] + [
        position + 1 for position in range(RADIUS)
    ]


def pair_weights(own_occ, near_occ, slot_list, used_count, tile_ids):
    tile_width = own_occ.shape[-1]
    used_mask = (
        jnp.arange(slot_list.shape[1], dtype=jnp.int32)[None, :] < used_count[:, None]
    ).astype(jnp.float32)
    itself = (slot_list == tile_ids[:, None]).astype(jnp.float32)
    identity_mask = jnp.eye(tile_width, dtype=jnp.float32)
    weight = used_mask[:, :, None, None] * own_occ[:, None, :, None] * near_occ[:, :, None, :]
    return weight * (1.0 - itself[:, :, None, None] * identity_mask[None, None])


def closeness(own_pos, near_pos):
    distance = jnp.zeros(near_pos.shape[:2] + (own_pos.shape[2], near_pos.shape[3]), jnp.float32)
    for coordinate in range(3):
        difference = own_pos[:, None, coordinate, :, None] - near_pos[:, :, coordinate, None, :]
        distance = distance + difference * difference
    return jnp.maximum(1.0 - distance / CUTOFF_SQUARE, 0.0)


def density_terms(own_pos, own_occ, near_pos, near_chi, near_occ, slot_list, used_count, tile_ids):
    weight = pair_weights(own_occ, near_occ, slot_list, used_count, tile_ids)
    within = closeness(own_pos, near_pos)
    reach_cube = weight * within * within * within
    density = jnp.sum(reach_cube * near_chi[:, :, None, :], axis=(1, 3))
    pair_energy = jnp.sum(reach_cube * within, axis=(1, 3))
    return (density, pair_energy)


def force_terms(
    own_pos,
    own_occ,
    own_chi,
    own_slope,
    near_pos,
    near_chi,
    near_occ,
    near_slope,
    slot_list,
    used_count,
    tile_ids,
):
    weight = pair_weights(own_occ, near_occ, slot_list, used_count, tile_ids)
    within = closeness(own_pos, near_pos)
    square = within * within
    mixed_slope = (
        own_slope[:, None, :, None] * near_chi[:, :, None, :]
        + near_slope[:, :, None, :] * own_chi[:, None, :, None]
    )
    pair_coef = (
        weight
        * (2.0 / CUTOFF_SQUARE)
        * (3.0 * square * mixed_slope + 4.0 * REPULSE * square * within)
    )
    total_coef = jnp.sum(pair_coef, axis=(1, 3))
    pulled = jnp.einsum("bpij,bpcj->bci", pair_coef, near_pos, precision=EXACT_PRODUCT)
    return own_pos * total_coef[:, None, :] - pulled


def add_counts(earlier, later):
    return earlier + later


def per_device(
    positions,
    velocity,
    density_weight,
    embed_strength,
    occupied,
    send_list,
    send_count,
    pair_tiles,
    pair_count,
    migrate_dest,
):
    tile_width = TILE
    tiles_here = pair_tiles.shape[0]
    ghost_most = send_list.shape[2]
    domains = lax.axis_size("dom")
    own_index = lax.axis_index("dom")
    strides = offset_list()
    filled = occupied.astype(jnp.float32).reshape(tiles_here, tile_width)
    pos_tiles = positions.reshape(3, tiles_here, tile_width).transpose(1, 0, 2)
    vel_tiles = velocity.reshape(3, tiles_here, tile_width).transpose(1, 0, 2)
    weight_tiles = density_weight.reshape(tiles_here, tile_width)
    embed_tiles = embed_strength.reshape(tiles_here, tile_width)
    packed = jnp.concatenate([pos_tiles, weight_tiles[:, None], filled[:, None]], axis=1)
    live_mask = (jnp.arange(ghost_most, dtype=jnp.int32)[None, :] < send_count[0][:, None]).astype(
        jnp.float32
    )
    blocks = packed[send_list[0]] * live_mask[:, :, None, None]
    ghosts = jnp.stack(
        [shifted(blocks[place], "dom", -stride) for place, stride in enumerate(strides)]
    )
    frame_tiles = jnp.concatenate([packed, ghosts.reshape(-1, 5, tile_width)], axis=0)
    block_size = math.gcd(tiles_here, 8)
    block_count = tiles_here // block_size
    tile_ids = jnp.arange(tiles_here, dtype=jnp.int32).reshape(block_count, block_size)
    packed_blocks = packed.reshape(block_count, block_size, 5, tile_width)
    slot_blocks = pair_tiles.reshape(block_count, block_size, pair_tiles.shape[1])
    used_blocks = pair_count.reshape(block_count, block_size)

    def density_block(batch_items):
        native, slot_list, used_count, block_ids = batch_items
        nearby = frame_tiles[slot_list]
        return density_terms(
            native[:, 0:3],
            native[:, 4],
            nearby[:, :, 0:3],
            nearby[:, :, 3],
            nearby[:, :, 4],
            slot_list,
            used_count,
            block_ids,
        )

    density, pair_energy = lax.map(
        density_block, (packed_blocks, slot_blocks, used_blocks, tile_ids)
    )
    density = density.reshape(tiles_here, tile_width)
    pair_energy = pair_energy.reshape(tiles_here, tile_width)
    root_term = jnp.sqrt(1.0 + density)
    slope_tiles = -0.5 * embed_tiles * filled / root_term
    energy_tiles = filled * (-embed_tiles * root_term + 0.5 * REPULSE * pair_energy)
    slope_blocks = slope_tiles[send_list[0]] * live_mask[:, :, None]
    ghost_slope = jnp.stack(
        [shifted(slope_blocks[place], "dom", -stride) for place, stride in enumerate(strides)]
    )
    slope_frame = jnp.concatenate([slope_tiles, ghost_slope.reshape(-1, tile_width)], axis=0)

    def force_block(batch_items):
        native, slot_list, used_count, block_ids, own_slope = batch_items
        nearby = frame_tiles[slot_list]
        near_slope = slope_frame[slot_list]
        return force_terms(
            native[:, 0:3],
            native[:, 4],
            native[:, 3],
            own_slope,
            nearby[:, :, 0:3],
            nearby[:, :, 3],
            nearby[:, :, 4],
            near_slope,
            slot_list,
            used_count,
            block_ids,
        )

    force_tiles = lax.map(
        force_block,
        (
            packed_blocks,
            slot_blocks,
            used_blocks,
            tile_ids,
            slope_tiles.reshape(block_count, block_size, tile_width),
        ),
    )
    force_tiles = force_tiles.reshape(tiles_here, 3, tile_width)
    new_vel = vel_tiles + TIME_STEP * force_tiles
    new_pos = pos_tiles + TIME_STEP * new_vel
    payload = jnp.concatenate([new_pos, new_vel, filled[:, None]], axis=1)
    onehot = (migrate_dest[:, None] == jnp.arange(domains, dtype=jnp.int32)[None, :]).astype(
        jnp.int32
    )
    sent_tiles = jnp.sum(onehot, axis=0)
    rank_within = jnp.sum(onehot * (jnp.cumsum(onehot, axis=0) - onehot), axis=1)
    start_slot = prefix(sent_tiles, "dom", add_counts, jnp.zeros_like(sent_tiles))
    capacity = tiles_here + 2 * RADIUS * MMAX
    staying = migrate_dest == own_index
    self_slot = jnp.where(staying, start_slot[own_index] + rank_within, capacity)
    moved_tiles = (
        jnp.zeros((capacity, 7, tile_width), jnp.float32).at[self_slot].set(payload, mode="drop")
    )
    slot_range = jnp.arange(MMAX, dtype=jnp.int32)
    relative = migrate_dest - own_index
    offset_index = jnp.where(relative < 0, relative + RADIUS, relative + RADIUS - 1)
    offset_index = jnp.where(staying, 2 * RADIUS, offset_index)
    outgoing = (
        jnp.zeros((2 * RADIUS, MMAX, 7, tile_width), jnp.float32)
        .at[offset_index, rank_within]
        .set(payload, mode="drop")
    )
    for place, stride in enumerate(strides):
        aim_index = jnp.clip(own_index + stride, 0, domains - 1)
        arrived, their_start, their_sent = shifted(
            (outgoing[place], start_slot[aim_index], sent_tiles[aim_index]), "dom", stride
        )
        slot_list = jnp.where(slot_range < their_sent, their_start + slot_range, capacity)
        moved_tiles = moved_tiles.at[slot_list].set(arrived, mode="drop")
    moved_count = jnp.sum(moved_tiles[:, 6, :]).astype(jnp.int32)[None]
    force = force_tiles.transpose(1, 0, 2).reshape(3, tiles_here * tile_width)
    energy = energy_tiles.reshape(tiles_here * tile_width)
    moved = moved_tiles.transpose(1, 0, 2).reshape(7, capacity * tile_width)
    return (force, energy, moved, moved_count)


def solution(mesh):
    placed = (
        P(None, "dom"),
        P(None, "dom"),
        P("dom"),
        P("dom"),
        P("dom"),
        P("dom", None, None),
        P("dom", None),
        P("dom", None),
        P("dom"),
        P("dom"),
    )
    return jax.shard_map(
        per_device,
        mesh=mesh,
        in_specs=placed,
        out_specs=(P(None, "dom"), P("dom"), P(None, "dom"), P("dom")),
        check_vma=False,
    )
```

profile of v0, /device:TPU:17, one launch (start us, length us, event | category | flops | bytes accessed | tf_op | source)
XLA Modules:
  0.0 430.1 jit_solution(763123593490520324)
XLA Ops:
  4.6 3.1 collective-permute-start
  7.8 4.0 collective-permute-start.1
  11.8 3.1 collective-permute-start.2
  14.9 2.8 collective-permute-start.3
  18.3 36.3 %all-reduce = s32[1024]{0:T(1024)S(1)} all-reduce(s32[1024]{0:T(1024)S(1)} %dynamic-update-slice), channel_id=2, replica_groups=mesh['dom'=32] {'dom'}, use_global_device_ids=true, to_apply=%add | all-reduce | flops 1024 | bytes 8192
  56.7 4.1 collective-permute-start.17
  63.5 2.9 collective-permute-start.16
  67.8 8.3 %collective-permute-start.20 = (s32[]{:T(128)}, s32[]{:T(128)}, u32[]{:S(2)}, u32[]{:S(2)}) collective-permute-start(s32[]{:T(128)} %bitcast.104), channel_id=1, source_target_pairs={{3,0},{4,1},{5,2},{6,3},{7,4},{8,5},{9,6},{10,7},{11,8},{12,9},{13... | collective-permute-start | bytes 20 | tf_op jit(solution)/shard_map/ppermute | solution.py:22
  78.0 4.9 %collective-permute-start.19 = (s32[]{:T(128)}, s32[]{:T(128)}, u32[]{:S(2)}, u32[]{:S(2)}) collective-permute-start(s32[]{:T(128)} %bitcast.103), channel_id=1, source_target_pairs={{3,0},{4,1},{5,2},{6,3},{7,4},{8,5},{9,6},{10,7},{11,8},{12,9},{13... | collective-permute-start | bytes 20 | tf_op jit(solution)/shard_map/ppermute | solution.py:22
  83.6 3.2 collective-permute-start.23
  88.6 4.4 %collective-permute-start.22 = (s32[]{:T(128)}, s32[]{:T(128)}, u32[]{:S(2)}, u32[]{:S(2)}) collective-permute-start(s32[]{:T(128)} %bitcast.107), channel_id=1, source_target_pairs={{2,0},{3,1},{4,2},{5,3},{6,4},{7,5},{8,6},{9,7},{10,8},{11,9},{12,... | collective-permute-start | bytes 20 | tf_op jit(solution)/shard_map/ppermute | solution.py:22
  94.0 6.6 %collective-permute-start.26 = (s32[]{:T(128)}, s32[]{:T(128)}, u32[]{:S(2)}, u32[]{:S(2)}) collective-permute-start(s32[]{:T(128)} %bitcast.112), channel_id=1, source_target_pairs={{1,0},{2,1},{3,2},{4,3},{5,4},{6,5},{7,6},{8,7},{9,8},{10,9},{11,1... | collective-permute-start | bytes 20 | tf_op jit(solution)/shard_map/ppermute | solution.py:22
  104.3 3.1 collective-permute-done.25
  112.4 2.5 collective-permute-start.28
  114.9 4.4 %collective-permute-done.28 = s32[]{:T(128)} collective-permute-done((s32[]{:T(128)}, s32[]{:T(128)}, u32[]{:S(2)}, u32[]{:S(2)}) %collective-permute-start.28) | collective-permute-done | bytes 36 | tf_op jit(solution)/shard_map/ppermute | solution.py:22
  123.1 2.7 collective-permute-done.32
  127.7 4.3 %collective-permute-done.31 = s32[]{:T(128)} collective-permute-done((s32[]{:T(128)}, s32[]{:T(128)}, u32[]{:S(2)}, u32[]{:S(2)}) %collective-permute-start.31) | collective-permute-done | bytes 36 | tf_op jit(solution)/shard_map/ppermute | solution.py:22
  132.0 3.8 collective-permute-start.35
  137.7 3.3 collective-permute-done.35
  142.9 5.1 %collective-permute-done.34 = s32[]{:T(128)} collective-permute-done((s32[]{:T(128)}, s32[]{:T(128)}, u32[]{:S(2)}, u32[]{:S(2)}) %collective-permute-start.34) | collective-permute-done | bytes 36 | tf_op jit(solution)/shard_map/ppermute | solution.py:22
  148.0 3.9 collective-permute-start.4
  155.7 4.9 %collective-permute-start.6 = (f32[8,5,128]{2,1,0:T(8,128)S(1)}, f32[8,5,128]{2,1,0:T(8,128)S(1)}, u32[]{:S(2)}, u32[]{:S(2)}) collective-permute-start(f32[8,5,128]{2,1,0:T(8,128)S(1)} %get-tuple-element.272), channel_id=1, source_target_pairs={{3,0},{4,1},{5,2},{6,3},{7,4},{8,5},{9,6},{10,7},{11,8},{12,9},{13... | collective-permute-start | bytes 61448 | tf_op jit(solution)/shard_map/ppermute | solution.py:22
  160.6 2.8 collective-permute-start.7
  163.4 2.5 collective-permute-start.38
  166.0 2.7 collective-permute-start.37
  168.8 51.5 %while.36 = (s32[]{:T(128)}, f32[4,8,128]{2,1,0:T(8,128)S(1)}, f32[4,8,128]{2,1,0:T(8,128)S(1)}, s32[4,8]{1,0:T(4,128)S(1)}, f32[4,8,5,128]{3,1,2,0:T(8,128)S(1)...) while((s32[]{:T(128)}, f32[4,8,128]{2,1,0:T(8,128)S(1)}, ...), condition=%wide.region_3.4_spmd, body=%wide.region_0.3_spmd.sunk | while | flops 69263680 | bytes 2912821 | solution.py:159
  170.5 11.1 %multiply_reduce_fusion.3 = (f32[8,128]{1,0:T(8,128)S(1)}, f32[8,128]{1,0:T(8,128)S(1)}) fusion(f32[8,24,128]{2,1,0:T(8,128)S(1)} %bitcast.333, f32[8,128]{1,0:T(8,128)S(1)} %get-tuple-element.454, f32[8,24,128]{2,1,0:T(8,128)S(1)} %bitcast.334, f32[8,128]{1,0:T(8,128)S(1)} %get-tuple-element.456, f32[8,24,128]{2,1,0:T(8,128)S(1)} %bitcast.335, ...), kind=kLoop, calls=%fused_computation.16.clone.1 | loop fusion | flops 69203968 | bytes 676608 | tf_op jit(solution)/shard_map/while/body/eval_jaxpr/reduce_sum | solution.py:68
  183.4 11.1 %multiply_reduce_fusion.3 = (f32[8,128]{1,0:T(8,128)S(1)}, f32[8,128]{1,0:T(8,128)S(1)}) fusion(f32[8,24,128]{2,1,0:T(8,128)S(1)} %bitcast.333, f32[8,128]{1,0:T(8,128)S(1)} %get-tuple-element.454, f32[8,24,128]{2,1,0:T(8,128)S(1)} %bitcast.334, f32[8,128]{1,0:T(8,128)S(1)} %get-tuple-element.456, f32[8,24,128]{2,1,0:T(8,128)S(1)} %bitcast.335, ...), kind=kLoop, calls=%fused_computation.16.clone.1 | loop fusion | flops 69203968 | bytes 676608 | tf_op jit(solution)/shard_map/while/body/eval_jaxpr/reduce_sum | solution.py:68
  196.3 11.1 %multiply_reduce_fusion.3 = (f32[8,128]{1,0:T(8,128)S(1)}, f32[8,128]{1,0:T(8,128)S(1)}) fusion(f32[8,24,128]{2,1,0:T(8,128)S(1)} %bitcast.333, f32[8,128]{1,0:T(8,128)S(1)} %get-tuple-element.454, f32[8,24,128]{2,1,0:T(8,128)S(1)} %bitcast.334, f32[8,128]{1,0:T(8,128)S(1)} %get-tuple-element.456, f32[8,24,128]{2,1,0:T(8,128)S(1)} %bitcast.335, ...), kind=kLoop, calls=%fused_computation.16.clone.1 | loop fusion | flops 69203968 | bytes 676608 | tf_op jit(solution)/shard_map/while/body/eval_jaxpr/reduce_sum | solution.py:68
  209.2 11.1 %multiply_reduce_fusion.3 = (f32[8,128]{1,0:T(8,128)S(1)}, f32[8,128]{1,0:T(8,128)S(1)}) fusion(f32[8,24,128]{2,1,0:T(8,128)S(1)} %bitcast.333, f32[8,128]{1,0:T(8,128)S(1)} %get-tuple-element.454, f32[8,24,128]{2,1,0:T(8,128)S(1)} %bitcast.334, f32[8,128]{1,0:T(8,128)S(1)} %get-tuple-element.456, f32[8,24,128]{2,1,0:T(8,128)S(1)} %bitcast.335, ...), kind=kLoop, calls=%fused_computation.16.clone.1 | loop fusion | flops 69203968 | bytes 676608 | tf_op jit(solution)/shard_map/while/body/eval_jaxpr/reduce_sum | solution.py:68
  225.8 2.5 collective-permute-start.10
  228.3 3.7 collective-permute-start.11
  234.0 4.3 collective-permute-start.13
  238.3 5.1 %collective-permute-start.14 = (f32[8,128]{1,0:T(8,128)S(1)}, f32[8,128]{1,0:T(8,128)S(1)}, u32[]{:S(2)}, u32[]{:S(2)}) collective-permute-start(f32[8,128]{1,0:T(8,128)S(1)} %get-tuple-element.288), channel_id=1, source_target_pairs={{3,0},{4,1},{5,2},{6,3},{7,4},{8,5},{9,6},{10,7},{11,8},{12,9},{13... | collective-permute-start | bytes 12296 | tf_op jit(solution)/shard_map/ppermute | solution.py:22
  243.4 3.9 collective-permute-start.15
  247.9 144.7 %while.37 = (s32[]{:T(128)}, f32[4,8,3,128]{3,2,1,0:T(4,128)S(1)}, f32[4,8,5,128]{3,2,1,0:T(8,128)S(1)}, s32[4,8]{1,0:T(4,128)S(1)}, s32[4,8,24]{2,1,0:T(8,128)S...) while((s32[]{:T(128)}, f32[4,8,3,128]{3,2,1,0:T(4,128)S(1)}, ...), condition=%wide.region_6.7_spmd, body=%wide.region_4.6_spmd.sunk | while | flops 280034624 | bytes 4420925 | solution.py:191
  250.3 13.2 %fusion.70 = f32[8,128]{1,0:T(8,128)S(1)} fusion(f32[8,128]{1,0:T(8,128)S(1)} %bitcast.343, f32[8,24,128]{2,1,0:T(8,128)S(1)} %bitcast.320, f32[8,24,128]{2,1,0:T(8,128)S(1)} %bitcast.324, f32[8,128]{1,0:T(8,128)S(1)} %dynamic-slice_bitcast_fusion.8, f32[8,24,128]{2,1,0:T(8,128)S(1)} %bitcast.326, f32[8,128]{1,0:T(8,128)S(1)} %bitcast.345, ...), kind=kLoop, calls=%fused_computation.41.clone.1 | loop fusion | flops 84933632 | bytes 779008 | tf_op jit(solution)/shard_map/while/body/eval_jaxpr/reduce_sum | solution.py:97
  263.5 20.5 %fusion.71 = f32[4,8,3,128]{3,2,1,0:T(4,128)S(1)} fusion(f32[4,8,3,128]{3,2,1,0:T(4,128)S(1)} %get-tuple-element.529, s32[]{:T(128)} %get-tuple-element.528, f32[8,128]{1,0:T(8,128)S(1)} %bitcast.344, f32[8,24,128]{2,1,0:T(8,128)S(1)} %bitcast.321, f32[8,24,128]{2,1,0:T(8,128)S(1)} %bitcast.325, f32[8,128]{1,0:T(8,128)S(1)} %dynamic-slice_bitcast_fusion.8, ...), kind=kOutput, calls=%fused_computation.45.clone.1 | convolution fusion | flops 195041280 | bytes 1208324 | tf_op jit(solution)/shard_map/while/body/eval_jaxpr/bpij,bpcj->bci/dot_general | solution.py:98
  286.4 13.2 %fusion.70 = f32[8,128]{1,0:T(8,128)S(1)} fusion(f32[8,128]{1,0:T(8,128)S(1)} %bitcast.343, f32[8,24,128]{2,1,0:T(8,128)S(1)} %bitcast.320, f32[8,24,128]{2,1,0:T(8,128)S(1)} %bitcast.324, f32[8,128]{1,0:T(8,128)S(1)} %dynamic-slice_bitcast_fusion.8, f32[8,24,128]{2,1,0:T(8,128)S(1)} %bitcast.326, f32[8,128]{1,0:T(8,128)S(1)} %bitcast.345, ...), kind=kLoop, calls=%fused_computation.41.clone.1 | loop fusion | flops 84933632 | bytes 779008 | tf_op jit(solution)/shard_map/while/body/eval_jaxpr/reduce_sum | solution.py:97
  299.6 20.5 %fusion.71 = f32[4,8,3,128]{3,2,1,0:T(4,128)S(1)} fusion(f32[4,8,3,128]{3,2,1,0:T(4,128)S(1)} %get-tuple-element.529, s32[]{:T(128)} %get-tuple-element.528, f32[8,128]{1,0:T(8,128)S(1)} %bitcast.344, f32[8,24,128]{2,1,0:T(8,128)S(1)} %bitcast.321, f32[8,24,128]{2,1,0:T(8,128)S(1)} %bitcast.325, f32[8,128]{1,0:T(8,128)S(1)} %dynamic-slice_bitcast_fusion.8, ...), kind=kOutput, calls=%fused_computation.45.clone.1 | convolution fusion | flops 195041280 | bytes 1208324 | tf_op jit(solution)/shard_map/while/body/eval_jaxpr/bpij,bpcj->bci/dot_general | solution.py:98
  322.6 13.2 %fusion.70 = f32[8,128]{1,0:T(8,128)S(1)} fusion(f32[8,128]{1,0:T(8,128)S(1)} %bitcast.343, f32[8,24,128]{2,1,0:T(8,128)S(1)} %bitcast.320, f32[8,24,128]{2,1,0:T(8,128)S(1)} %bitcast.324, f32[8,128]{1,0:T(8,128)S(1)} %dynamic-slice_bitcast_fusion.8, f32[8,24,128]{2,1,0:T(8,128)S(1)} %bitcast.326, f32[8,128]{1,0:T(8,128)S(1)} %bitcast.345, ...), kind=kLoop, calls=%fused_computation.41.clone.1 | loop fusion | flops 84933632 | bytes 779008 | tf_op jit(solution)/shard_map/while/body/eval_jaxpr/reduce_sum | solution.py:97
  335.8 20.5 %fusion.71 = f32[4,8,3,128]{3,2,1,0:T(4,128)S(1)} fusion(f32[4,8,3,128]{3,2,1,0:T(4,128)S(1)} %get-tuple-element.529, s32[]{:T(128)} %get-tuple-element.528, f32[8,128]{1,0:T(8,128)S(1)} %bitcast.344, f32[8,24,128]{2,1,0:T(8,128)S(1)} %bitcast.321, f32[8,24,128]{2,1,0:T(8,128)S(1)} %bitcast.325, f32[8,128]{1,0:T(8,128)S(1)} %dynamic-slice_bitcast_fusion.8, ...), kind=kOutput, calls=%fused_computation.45.clone.1 | convolution fusion | flops 195041280 | bytes 1208324 | tf_op jit(solution)/shard_map/while/body/eval_jaxpr/bpij,bpcj->bci/dot_general | solution.py:98
  358.7 13.2 %fusion.70 = f32[8,128]{1,0:T(8,128)S(1)} fusion(f32[8,128]{1,0:T(8,128)S(1)} %bitcast.343, f32[8,24,128]{2,1,0:T(8,128)S(1)} %bitcast.320, f32[8,24,128]{2,1,0:T(8,128)S(1)} %bitcast.324, f32[8,128]{1,0:T(8,128)S(1)} %dynamic-slice_bitcast_fusion.8, f32[8,24,128]{2,1,0:T(8,128)S(1)} %bitcast.326, f32[8,128]{1,0:T(8,128)S(1)} %bitcast.345, ...), kind=kLoop, calls=%fused_computation.41.clone.1 | loop fusion | flops 84933632 | bytes 779008 | tf_op jit(solution)/shard_map/while/body/eval_jaxpr/reduce_sum | solution.py:97
  371.9 20.5 %fusion.71 = f32[4,8,3,128]{3,2,1,0:T(4,128)S(1)} fusion(f32[4,8,3,128]{3,2,1,0:T(4,128)S(1)} %get-tuple-element.529, s32[]{:T(128)} %get-tuple-element.528, f32[8,128]{1,0:T(8,128)S(1)} %bitcast.344, f32[8,24,128]{2,1,0:T(8,128)S(1)} %bitcast.321, f32[8,24,128]{2,1,0:T(8,128)S(1)} %bitcast.325, f32[8,128]{1,0:T(8,128)S(1)} %dynamic-slice_bitcast_fusion.8, ...), kind=kOutput, calls=%fused_computation.45.clone.1 | convolution fusion | flops 195041280 | bytes 1208324 | tf_op jit(solution)/shard_map/while/body/eval_jaxpr/bpij,bpcj->bci/dot_general | solution.py:98
  394.8 4.5 %collective-permute-start.18 = (f32[4,7,128]{2,1,0:T(8,128)S(1)}, f32[4,7,128]{2,1,0:T(8,128)S(1)}, u32[]{:S(2)}, u32[]{:S(2)}) collective-permute-start(f32[4,7,128]{2,1,0:T(8,128)S(1)} %get-tuple-element.286), channel_id=1, source_target_pairs={{4,0},{5,1},{6,2},{7,3},{8,4},{9,5},{10,6},{11,7},{12,8},{13,9},{1... | collective-permute-start | bytes 43016 | tf_op jit(solution)/shard_map/ppermute | solution.py:22
  407.4 3.5 collective-permute-start.30
  411.0 3.9 collective-permute-start.33
  416.8 3.3 collective-permute-start.39
  (324 shorter events, 82.3 us)
Async XLA Ops:
  1.4 167.4 %copy-start.4 = (f32[4096]{0:T(1024)}, f32[4096]{0:T(1024)S(1)}, u32[]{:S(2)}) copy-start(f32[4096]{0:T(1024)S(1)} %convert_element_type.62) | copy-start | bytes 49156
  4.4 57.2 %copy-start.1 = (f32[3,4096]{1,0:T(4,128)S(1)}, f32[3,4096]{1,0:T(4,128)}, u32[]{:S(2)}) copy-start(f32[3,4096]{1,0:T(4,128)} %param.16) | copy-start | bytes 147460
  4.4 57.1 %copy-start.8 = (f32[4096]{0:T(1024)S(1)}, f32[4096]{0:T(1024)}, u32[]{:S(2)}) copy-start(f32[4096]{0:T(1024)} %param.18) | copy-start | bytes 49156
  4.6 57.1 %copy-start.27 = (s32[32]{0:T(128)S(1)}, s32[32]{0:T(128)}, u32[]{:S(2)}) copy-start(s32[32]{0:T(128)} %param.24) | copy-start | bytes 388
  4.6 149.1 %collective-permute-start = (f32[8,5,128]{2,1,0:T(8,128)S(1)}, f32[8,5,128]{2,1,0:T(8,128)S(1)}, u32[]{:S(2)}, u32[]{:S(2)}) collective-permute-start(f32[8,5,128]{2,1,0:T(8,128)S(1)} %get-tuple-element.278), channel_id=1, source_target_pairs={{0,4},{1,5},{2,6},{3,7},{4,8},{5,9},{6,10},{7,11},{8,12},{9,13},{1... | collective-permute-start | bytes 61448 | tf_op jit(solution)/shard_map/ppermute | solution.py:22
  7.8 147.9 %collective-permute-start.1 = (f32[8,5,128]{2,1,0:T(8,128)S(1)}, f32[8,5,128]{2,1,0:T(8,128)S(1)}, u32[]{:S(2)}, u32[]{:S(2)}) collective-permute-start(f32[8,5,128]{2,1,0:T(8,128)S(1)} %get-tuple-element.277), channel_id=1, source_target_pairs={{0,3},{1,4},{2,5},{3,6},{4,7},{5,8},{6,9},{7,10},{8,11},{9,12},{10... | collective-permute-start | bytes 61448 | tf_op jit(solution)/shard_map/ppermute | solution.py:22
  11.8 148.8 %collective-permute-start.2 = (f32[8,5,128]{2,1,0:T(8,128)S(1)}, f32[8,5,128]{2,1,0:T(8,128)S(1)}, u32[]{:S(2)}, u32[]{:S(2)}) collective-permute-start(f32[8,5,128]{2,1,0:T(8,128)S(1)} %get-tuple-element.276), channel_id=1, source_target_pairs={{0,2},{1,3},{2,4},{3,5},{4,6},{5,7},{6,8},{7,9},{8,10},{9,11},{10,... | collective-permute-start | bytes 61448 | tf_op jit(solution)/shard_map/ppermute | solution.py:22
  14.9 148.5 %collective-permute-start.3 = (f32[8,5,128]{2,1,0:T(8,128)S(1)}, f32[8,5,128]{2,1,0:T(8,128)S(1)}, u32[]{:S(2)}, u32[]{:S(2)}) collective-permute-start(f32[8,5,128]{2,1,0:T(8,128)S(1)} %get-tuple-element.275), channel_id=1, source_target_pairs={{0,1},{1,2},{2,3},{3,4},{4,5},{5,6},{6,7},{7,8},{8,9},{9,10},{10,1... | collective-permute-start | bytes 61448 | tf_op jit(solution)/shard_map/ppermute | solution.py:22
  56.7 6.8 %collective-permute-start.17 = (s32[]{:T(128)}, s32[]{:T(128)}, u32[]{:S(2)}, u32[]{:S(2)}) collective-permute-start(s32[]{:T(128)} %bitcast.97), channel_id=1, source_target_pairs={{4,0},{5,1},{6,2},{7,3},{8,4},{9,5},{10,6},{11,7},{12,8},{13,9},{1... | collective-permute-start | bytes 20 | tf_op jit(solution)/shard_map/ppermute | solution.py:22
  63.5 4.3 %collective-permute-start.16 = (s32[]{:T(128)}, s32[]{:T(128)}, u32[]{:S(2)}, u32[]{:S(2)}) collective-permute-start(s32[]{:T(128)} %bitcast.96), channel_id=1, source_target_pairs={{4,0},{5,1},{6,2},{7,3},{8,4},{9,5},{10,6},{11,7},{12,8},{13,9},{1... | collective-permute-start | bytes 20 | tf_op jit(solution)/shard_map/ppermute | solution.py:22
  67.8 10.2 %collective-permute-start.20 = (s32[]{:T(128)}, s32[]{:T(128)}, u32[]{:S(2)}, u32[]{:S(2)}) collective-permute-start(s32[]{:T(128)} %bitcast.104), channel_id=1, source_target_pairs={{3,0},{4,1},{5,2},{6,3},{7,4},{8,5},{9,6},{10,7},{11,8},{12,9},{13... | collective-permute-start | bytes 20 | tf_op jit(solution)/shard_map/ppermute | solution.py:22
  78.0 5.6 %collective-permute-start.19 = (s32[]{:T(128)}, s32[]{:T(128)}, u32[]{:S(2)}, u32[]{:S(2)}) collective-permute-start(s32[]{:T(128)} %bitcast.103), channel_id=1, source_target_pairs={{3,0},{4,1},{5,2},{6,3},{7,4},{8,5},{9,6},{10,7},{11,8},{12,9},{13... | collective-permute-start | bytes 20 | tf_op jit(solution)/shard_map/ppermute | solution.py:22
  83.6 5.0 %collective-permute-start.23 = (s32[]{:T(128)}, s32[]{:T(128)}, u32[]{:S(2)}, u32[]{:S(2)}) collective-permute-start(s32[]{:T(128)} %bitcast.108), channel_id=1, source_target_pairs={{2,0},{3,1},{4,2},{5,3},{6,4},{7,5},{8,6},{9,7},{10,8},{11,9},{12,... | collective-permute-start | bytes 20 | tf_op jit(solution)/shard_map/ppermute | solution.py:22
  88.6 5.3 %collective-permute-start.22 = (s32[]{:T(128)}, s32[]{:T(128)}, u32[]{:S(2)}, u32[]{:S(2)}) collective-permute-start(s32[]{:T(128)} %bitcast.107), channel_id=1, source_target_pairs={{2,0},{3,1},{4,2},{5,3},{6,4},{7,5},{8,6},{9,7},{10,8},{11,9},{12,... | collective-permute-start | bytes 20 | tf_op jit(solution)/shard_map/ppermute | solution.py:22
  94.0 8.4 %collective-permute-start.26 = (s32[]{:T(128)}, s32[]{:T(128)}, u32[]{:S(2)}, u32[]{:S(2)}) collective-permute-start(s32[]{:T(128)} %bitcast.112), channel_id=1, source_target_pairs={{1,0},{2,1},{3,2},{4,3},{5,4},{6,5},{7,6},{8,7},{9,8},{10,9},{11,1... | collective-permute-start | bytes 20 | tf_op jit(solution)/shard_map/ppermute | solution.py:22
  102.4 5.0 %collective-permute-start.25 = (s32[]{:T(128)}, s32[]{:T(128)}, u32[]{:S(2)}, u32[]{:S(2)}) collective-permute-start(s32[]{:T(128)} %bitcast.111), channel_id=1, source_target_pairs={{1,0},{2,1},{3,2},{4,3},{5,4},{6,5},{7,6},{8,7},{9,8},{10,9},{11,1... | collective-permute-start | bytes 20 | tf_op jit(solution)/shard_map/ppermute | solution.py:22
  107.5 4.9 %collective-permute-start.29 = (s32[]{:T(128)}, s32[]{:T(128)}, u32[]{:S(2)}, u32[]{:S(2)}) collective-permute-start(s32[]{:T(128)} %bitcast.116), channel_id=1, source_target_pairs={{0,1},{1,2},{2,3},{3,4},{4,5},{5,6},{6,7},{7,8},{8,9},{9,10},{10,1... | collective-permute-start | bytes 20 | tf_op jit(solution)/shard_map/ppermute | solution.py:22
  112.4 6.9 %collective-permute-start.28 = (s32[]{:T(128)}, s32[]{:T(128)}, u32[]{:S(2)}, u32[]{:S(2)}) collective-permute-start(s32[]{:T(128)} %bitcast.115), channel_id=1, source_target_pairs={{0,1},{1,2},{2,3},{3,4},{4,5},{5,6},{6,7},{7,8},{8,9},{9,10},{10,1... | collective-permute-start | bytes 20 | tf_op jit(solution)/shard_map/ppermute | solution.py:22
  119.3 6.5 %collective-permute-start.32 = (s32[]{:T(128)}, s32[]{:T(128)}, u32[]{:S(2)}, u32[]{:S(2)}) collective-permute-start(s32[]{:T(128)} %bitcast.120), channel_id=1, source_target_pairs={{0,2},{1,3},{2,4},{3,5},{4,6},{5,7},{6,8},{7,9},{8,10},{9,11},{10,... | collective-permute-start | bytes 20 | tf_op jit(solution)/shard_map/ppermute | solution.py:22
  125.7 6.3 %collective-permute-start.31 = (s32[]{:T(128)}, s32[]{:T(128)}, u32[]{:S(2)}, u32[]{:S(2)}) collective-permute-start(s32[]{:T(128)} %bitcast.119), channel_id=1, source_target_pairs={{0,2},{1,3},{2,4},{3,5},{4,6},{5,7},{6,8},{7,9},{8,10},{9,11},{10,... | collective-permute-start | bytes 20 | tf_op jit(solution)/shard_map/ppermute | solution.py:22
  132.0 9.0 %collective-permute-start.35 = (s32[]{:T(128)}, s32[]{:T(128)}, u32[]{:S(2)}, u32[]{:S(2)}) collective-permute-start(s32[]{:T(128)} %bitcast.124), channel_id=1, source_target_pairs={{0,3},{1,4},{2,5},{3,6},{4,7},{5,8},{6,9},{7,10},{8,11},{9,12},{10... | collective-permute-start | bytes 20 | tf_op jit(solution)/shard_map/ppermute | solution.py:22
  141.0 7.0 %collective-permute-start.34 = (s32[]{:T(128)}, s32[]{:T(128)}, u32[]{:S(2)}, u32[]{:S(2)}) collective-permute-start(s32[]{:T(128)} %bitcast.123), channel_id=1, source_target_pairs={{0,3},{1,4},{2,5},{3,6},{4,7},{5,8},{6,9},{7,10},{8,11},{9,12},{10... | collective-permute-start | bytes 20 | tf_op jit(solution)/shard_map/ppermute | solution.py:22
  148.0 18.0 %collective-permute-start.4 = (f32[8,5,128]{2,1,0:T(8,128)S(1)}, f32[8,5,128]{2,1,0:T(8,128)S(1)}, u32[]{:S(2)}, u32[]{:S(2)}) collective-permute-start(f32[8,5,128]{2,1,0:T(8,128)S(1)} %get-tuple-element.274), channel_id=1, source_target_pairs={{1,0},{2,1},{3,2},{4,3},{5,4},{6,5},{7,6},{8,7},{9,8},{10,9},{11,1... | collective-permute-start | bytes 61448 | tf_op jit(solution)/shard_map/ppermute | solution.py:22
  153.8 14.9 %collective-permute-start.5 = (f32[8,5,128]{2,1,0:T(8,128)S(1)}, f32[8,5,128]{2,1,0:T(8,128)S(1)}, u32[]{:S(2)}, u32[]{:S(2)}) collective-permute-start(f32[8,5,128]{2,1,0:T(8,128)S(1)} %get-tuple-element.273), channel_id=1, source_target_pairs={{2,0},{3,1},{4,2},{5,3},{6,4},{7,5},{8,6},{9,7},{10,8},{11,9},{12,... | collective-permute-start | bytes 61448 | tf_op jit(solution)/shard_map/ppermute | solution.py:22
  155.7 13.0 %collective-permute-start.6 = (f32[8,5,128]{2,1,0:T(8,128)S(1)}, f32[8,5,128]{2,1,0:T(8,128)S(1)}, u32[]{:S(2)}, u32[]{:S(2)}) collective-permute-start(f32[8,5,128]{2,1,0:T(8,128)S(1)} %get-tuple-element.272), channel_id=1, source_target_pairs={{3,0},{4,1},{5,2},{6,3},{7,4},{8,5},{9,6},{10,7},{11,8},{12,9},{13... | collective-permute-start | bytes 61448 | tf_op jit(solution)/shard_map/ppermute | solution.py:22
  160.6 8.1 %collective-permute-start.7 = (f32[8,5,128]{2,1,0:T(8,128)S(1)}, f32[8,5,128]{2,1,0:T(8,128)S(1)}, u32[]{:S(2)}, u32[]{:S(2)}) collective-permute-start(f32[8,5,128]{2,1,0:T(8,128)S(1)} %get-tuple-element.271), channel_id=1, source_target_pairs={{4,0},{5,1},{6,2},{7,3},{8,4},{9,5},{10,6},{11,7},{12,8},{13,9},{1... | collective-permute-start | bytes 61448 | tf_op jit(solution)/shard_map/ppermute | solution.py:22
  163.4 240.7 %collective-permute-start.38 = (s32[]{:T(128)}, s32[]{:T(128)}, u32[]{:S(2)}, u32[]{:S(2)}) collective-permute-start(s32[]{:T(128)} %bitcast.128), channel_id=1, source_target_pairs={{0,4},{1,5},{2,6},{3,7},{4,8},{5,9},{6,10},{7,11},{8,12},{9,13},{1... | collective-permute-start | bytes 20 | tf_op jit(solution)/shard_map/ppermute | solution.py:22
  166.0 238.2 %collective-permute-start.37 = (s32[]{:T(128)}, s32[]{:T(128)}, u32[]{:S(2)}, u32[]{:S(2)}) collective-permute-start(s32[]{:T(128)} %bitcast.127), channel_id=1, source_target_pairs={{0,4},{1,5},{2,6},{3,7},{4,8},{5,9},{6,10},{7,11},{8,12},{9,13},{1... | collective-permute-start | bytes 20 | tf_op jit(solution)/shard_map/ppermute | solution.py:22
  221.1 7.3 %collective-permute-start.8 = (f32[8,128]{1,0:T(8,128)S(1)}, f32[8,128]{1,0:T(8,128)S(1)}, u32[]{:S(2)}, u32[]{:S(2)}) collective-permute-start(f32[8,128]{1,0:T(8,128)S(1)} %get-tuple-element.294), channel_id=1, source_target_pairs={{0,4},{1,5},{2,6},{3,7},{4,8},{5,9},{6,10},{7,11},{8,12},{9,13},{1... | collective-permute-start | bytes 12296 | tf_op jit(solution)/shard_map/ppermute | solution.py:22
  223.6 8.4 %collective-permute-start.9 = (f32[8,128]{1,0:T(8,128)S(1)}, f32[8,128]{1,0:T(8,128)S(1)}, u32[]{:S(2)}, u32[]{:S(2)}) collective-permute-start(f32[8,128]{1,0:T(8,128)S(1)} %get-tuple-element.293), channel_id=1, source_target_pairs={{0,3},{1,4},{2,5},{3,6},{4,7},{5,8},{6,9},{7,10},{8,11},{9,12},{10... | collective-permute-start | bytes 12296 | tf_op jit(solution)/shard_map/ppermute | solution.py:22
  225.8 8.2 %collective-permute-start.10 = (f32[8,128]{1,0:T(8,128)S(1)}, f32[8,128]{1,0:T(8,128)S(1)}, u32[]{:S(2)}, u32[]{:S(2)}) collective-permute-start(f32[8,128]{1,0:T(8,128)S(1)} %get-tuple-element.292), channel_id=1, source_target_pairs={{0,2},{1,3},{2,4},{3,5},{4,6},{5,7},{6,8},{7,9},{8,10},{9,11},{10,... | collective-permute-start | bytes 12296 | tf_op jit(solution)/shard_map/ppermute | solution.py:22
  228.3 9.9 %collective-permute-start.11 = (f32[8,128]{1,0:T(8,128)S(1)}, f32[8,128]{1,0:T(8,128)S(1)}, u32[]{:S(2)}, u32[]{:S(2)}) collective-permute-start(f32[8,128]{1,0:T(8,128)S(1)} %get-tuple-element.291), channel_id=1, source_target_pairs={{0,1},{1,2},{2,3},{3,4},{4,5},{5,6},{6,7},{7,8},{8,9},{9,10},{10,1... | collective-permute-start | bytes 12296 | tf_op jit(solution)/shard_map/ppermute | solution.py:22
  232.0 11.4 %collective-permute-start.12 = (f32[8,128]{1,0:T(8,128)S(1)}, f32[8,128]{1,0:T(8,128)S(1)}, u32[]{:S(2)}, u32[]{:S(2)}) collective-permute-start(f32[8,128]{1,0:T(8,128)S(1)} %get-tuple-element.290), channel_id=1, source_target_pairs={{1,0},{2,1},{3,2},{4,3},{5,4},{6,5},{7,6},{8,7},{9,8},{10,9},{11,1... | collective-permute-start | bytes 12296 | tf_op jit(solution)/shard_map/ppermute | solution.py:22
  234.0 13.3 %collective-permute-start.13 = (f32[8,128]{1,0:T(8,128)S(1)}, f32[8,128]{1,0:T(8,128)S(1)}, u32[]{:S(2)}, u32[]{:S(2)}) collective-permute-start(f32[8,128]{1,0:T(8,128)S(1)} %get-tuple-element.289), channel_id=1, source_target_pairs={{2,0},{3,1},{4,2},{5,3},{6,4},{7,5},{8,6},{9,7},{10,8},{11,9},{12,... | collective-permute-start | bytes 12296 | tf_op jit(solution)/shard_map/ppermute | solution.py:22
  238.3 9.0 %collective-permute-start.14 = (f32[8,128]{1,0:T(8,128)S(1)}, f32[8,128]{1,0:T(8,128)S(1)}, u32[]{:S(2)}, u32[]{:S(2)}) collective-permute-start(f32[8,128]{1,0:T(8,128)S(1)} %get-tuple-element.288), channel_id=1, source_target_pairs={{3,0},{4,1},{5,2},{6,3},{7,4},{8,5},{9,6},{10,7},{11,8},{12,9},{13... | collective-permute-start | bytes 12296 | tf_op jit(solution)/shard_map/ppermute | solution.py:22
  243.4 4.4 %collective-permute-start.15 = (f32[8,128]{1,0:T(8,128)S(1)}, f32[8,128]{1,0:T(8,128)S(1)}, u32[]{:S(2)}, u32[]{:S(2)}) collective-permute-start(f32[8,128]{1,0:T(8,128)S(1)} %get-tuple-element.287), channel_id=1, source_target_pairs={{4,0},{5,1},{6,2},{7,3},{8,4},{9,5},{10,6},{11,7},{12,8},{13,9},{1... | collective-permute-start | bytes 12296 | tf_op jit(solution)/shard_map/ppermute | solution.py:22
  247.8 144.8 %copy-start.2 = (f32[3,4096]{1,0:T(4,128)S(1)}, f32[3,4096]{1,0:T(4,128)}, u32[]{:S(2)}) copy-start(f32[3,4096]{1,0:T(4,128)} %param.16) | copy-start | bytes 147460
  247.9 144.8 %copy-start.13 = (f32[3,4096]{1,0:T(4,128)S(1)}, f32[3,4096]{1,0:T(4,128)}, u32[]{:S(2)}) copy-start(f32[3,4096]{1,0:T(4,128)} %param.17) | copy-start | bytes 147460
  247.9 144.9 %copy-start.5 = (f32[4096]{0:T(1024)S(1)}, f32[4096]{0:T(1024)}, u32[]{:S(2)}) copy-start(f32[4096]{0:T(1024)} %copy-done.4) | copy-start | bytes 49156
  247.9 145.0 %copy-start.3 = (s32[32]{0:T(128)S(1)}, s32[32]{0:T(128)}, u32[]{:S(2)}) copy-start(s32[32]{0:T(128)} %fusion.36) | copy-start | bytes 388
  394.8 16.1 %collective-permute-start.18 = (f32[4,7,128]{2,1,0:T(8,128)S(1)}, f32[4,7,128]{2,1,0:T(8,128)S(1)}, u32[]{:S(2)}, u32[]{:S(2)}) collective-permute-start(f32[4,7,128]{2,1,0:T(8,128)S(1)} %get-tuple-element.286), channel_id=1, source_target_pairs={{4,0},{5,1},{6,2},{7,3},{8,4},{9,5},{10,6},{11,7},{12,8},{13,9},{1... | collective-permute-start | bytes 43016 | tf_op jit(solution)/shard_map/ppermute | solution.py:22
  399.3 15.5 %collective-permute-start.21 = (f32[4,7,128]{2,1,0:T(8,128)S(1)}, f32[4,7,128]{2,1,0:T(8,128)S(1)}, u32[]{:S(2)}, u32[]{:S(2)}) collective-permute-start(f32[4,7,128]{2,1,0:T(8,128)S(1)} %get-tuple-element.285), channel_id=1, source_target_pairs={{3,0},{4,1},{5,2},{6,3},{7,4},{8,5},{9,6},{10,7},{11,8},{12,9},{13... | collective-permute-start | bytes 43016 | tf_op jit(solution)/shard_map/ppermute | solution.py:22
  401.8 15.0 %collective-permute-start.24 = (f32[4,7,128]{2,1,0:T(8,128)S(1)}, f32[4,7,128]{2,1,0:T(8,128)S(1)}, u32[]{:S(2)}, u32[]{:S(2)}) collective-permute-start(f32[4,7,128]{2,1,0:T(8,128)S(1)} %get-tuple-element.284), channel_id=1, source_target_pairs={{2,0},{3,1},{4,2},{5,3},{6,4},{7,5},{8,6},{9,7},{10,8},{11,9},{12,... | collective-permute-start | bytes 43016 | tf_op jit(solution)/shard_map/ppermute | solution.py:22
  405.4 19.0 %collective-permute-start.27 = (f32[4,7,128]{2,1,0:T(8,128)S(1)}, f32[4,7,128]{2,1,0:T(8,128)S(1)}, u32[]{:S(2)}, u32[]{:S(2)}) collective-permute-start(f32[4,7,128]{2,1,0:T(8,128)S(1)} %get-tuple-element.283), channel_id=1, source_target_pairs={{1,0},{2,1},{3,2},{4,3},{5,4},{6,5},{7,6},{8,7},{9,8},{10,9},{11,1... | collective-permute-start | bytes 43016 | tf_op jit(solution)/shard_map/ppermute | solution.py:22
  407.4 17.6 %collective-permute-start.30 = (f32[4,7,128]{2,1,0:T(8,128)S(1)}, f32[4,7,128]{2,1,0:T(8,128)S(1)}, u32[]{:S(2)}, u32[]{:S(2)}) collective-permute-start(f32[4,7,128]{2,1,0:T(8,128)S(1)} %get-tuple-element.282), channel_id=1, source_target_pairs={{0,1},{1,2},{2,3},{3,4},{4,5},{5,6},{6,7},{7,8},{8,9},{9,10},{10,1... | collective-permute-start | bytes 43016 | tf_op jit(solution)/shard_map/ppermute | solution.py:22
  411.0 14.7 %collective-permute-start.33 = (f32[4,7,128]{2,1,0:T(8,128)S(1)}, f32[4,7,128]{2,1,0:T(8,128)S(1)}, u32[]{:S(2)}, u32[]{:S(2)}) collective-permute-start(f32[4,7,128]{2,1,0:T(8,128)S(1)} %get-tuple-element.281), channel_id=1, source_target_pairs={{0,2},{1,3},{2,4},{3,5},{4,6},{5,7},{6,8},{7,9},{8,10},{9,11},{10,... | collective-permute-start | bytes 43016 | tf_op jit(solution)/shard_map/ppermute | solution.py:22
  414.9 11.5 %collective-permute-start.36 = (f32[4,7,128]{2,1,0:T(8,128)S(1)}, f32[4,7,128]{2,1,0:T(8,128)S(1)}, u32[]{:S(2)}, u32[]{:S(2)}) collective-permute-start(f32[4,7,128]{2,1,0:T(8,128)S(1)} %get-tuple-element.280), channel_id=1, source_target_pairs={{0,3},{1,4},{2,5},{3,6},{4,7},{5,8},{6,9},{7,10},{8,11},{9,12},{10... | collective-permute-start | bytes 43016 | tf_op jit(solution)/shard_map/ppermute | solution.py:22
  416.8 10.2 %collective-permute-start.39 = (f32[4,7,128]{2,1,0:T(8,128)S(1)}, f32[4,7,128]{2,1,0:T(8,128)S(1)}, u32[]{:S(2)}, u32[]{:S(2)}) collective-permute-start(f32[4,7,128]{2,1,0:T(8,128)S(1)} %get-tuple-element.279), channel_id=1, source_target_pairs={{0,4},{1,5},{2,6},{3,7},{4,8},{5,9},{6,10},{7,11},{8,12},{9,13},{1... | collective-permute-start | bytes 43016 | tf_op jit(solution)/shard_map/ppermute | solution.py:22
  (20 other events, 617.5 us)
where the time goes:
time: 434 us; the launch traced here: 430 us
  starting transfers between devices  132 us (30%)
  other arithmetic  121 us (28%)
  matrix products  82.1 us (19%)
  blocking collectives  36.3 us (8%)
  waiting for transfers between devices  27.8 us (6%)
  local copies, waits for them, and re-layouts  25.8 us (6%)
    ppermute x40, starting transfers between devices, shifted(): return lax.ppermute(block, axis, route)  132 us
    dot_general x4, matrix products, force_terms(): jnp.einsum('bpij,bpcj->bci', pair_coef, near_pos, precision=EXACT_PRODUCT)  82.1 us
    reduce_sum x4, other arithmetic, force_terms(): total_coef = jnp.sum(pair_coef, axis=(1, 3))  52.8 us
    reduce_sum x4, other arithmetic, density_terms(): pair_energy = jnp.sum(reach_cube * within, axis=(1, 3))  44.6 us
    unnamed x1, blocking collectives  36.3 us
    ppermute x40, waiting for transfers between devices, shifted(): return lax.ppermute(block, axis, route)  27.8 us
    select_n x8, other arithmetic, per_device(): moved_tiles = moved_tiles.at[slot_list].set(arrived, mode='drop')  14.1 us
  transfers between devices with their start and end apart: 40, of which 11 were waited for; matrix products, arithmetic and copies ran while one was open for 52% of the time, Pallas kernels for 0%

commit v1 on v0

v1 whole, which is shorter than its diff:
```python
import functools

import jax
import jax.numpy as jnp
from jax import lax
from jax.experimental import pallas as pl
from jax.experimental.pallas import tpu as pltpu
from jax.sharding import PartitionSpec as P

TILE = 128
RADIUS = 4
MMAX = 4
REPULSE = 0.05
TIME_STEP = 0.05
FAR = 1e15
MESH = pl.DeviceIdType.MESH
OFFSETS = [position - RADIUS for position in range(RADIUS)] + [
    position + 1 for position in range(RADIUS)
]
VMEM = pl.BlockSpec(memory_space=pltpu.VMEM)
SMEM = pl.BlockSpec(memory_space=pltpu.SMEM)
ANY = pl.BlockSpec(memory_space=pl.ANY)
WIDE = 60 * 1024 * 1024


def exists(device, domains):
    return jnp.logical_and(device >= 0, device < domains)


def greet(me, domains):
    barrier = pltpu.get_barrier_semaphore()
    for offset in OFFSETS:

        @pl.when(exists(me + offset, domains))
        def _():
            pl.semaphore_signal(
                barrier, inc=1, device_id=(me + offset,), device_id_type=MESH
            )

    peers = jnp.minimum(me, RADIUS) + jnp.minimum(domains - 1 - me, RADIUS)
    pl.semaphore_wait(barrier, peers)


def frame_kernel(
    domains,
    send_list,
    send_count,
    positions,
    density,
    occupied,
    dest,
    own,
    ghost,
    dests,
    outbox,
    dest_row,
    send_sem,
    recv_sem,
    dest_send,
    dest_recv,
):
    me = lax.axis_index("dom")
    tiles = own.shape[0]
    ghosts = send_list.shape[2]
    filled = occupied[...].astype(jnp.float32)
    weight = density[...] * filled
    own[...] = jnp.zeros_like(own)
    for t in range(tiles):
        here = filled[t : t + 1, :]
        for c in range(3):
            own[t, c : c + 1, :] = jnp.where(
                here > 0, 0.5 * positions[c : c + 1, t * TILE : (t + 1) * TILE], FAR
            )
        own[t, 3:4, :] = weight[t : t + 1, :]
        own[t, 4:5, :] = here
    dest_row[...] = jnp.full_like(dest_row, -1)
    dest_row[:, 0:tiles] = dest[...]
    row = lax.broadcasted_iota(jnp.int32, (8, TILE), 0)
    empty = jnp.where(row < 3, FAR, 0.0)
    for k in range(len(OFFSETS)):
        used = send_count[0, k]
        for g in range(ghosts):
            outbox[k, g] = jnp.where(g < used, own[send_list[0, k, g]], empty)
    greet(me, domains)
    for k, offset in enumerate(OFFSETS):

        @pl.when(exists(me - offset, domains))
        def _():
            pltpu.make_async_remote_copy(
                src_ref=outbox.at[k],
                dst_ref=ghost.at[k],
                send_sem=send_sem.at[k],
                recv_sem=recv_sem.at[k],
                device_id=(me - offset,),
                device_id_type=MESH,
            ).start()
            pltpu.make_async_remote_copy(
                src_ref=dest_row,
                dst_ref=dests.at[k],
                send_sem=dest_send.at[k],
                recv_sem=dest_recv.at[k],
                device_id=(me - offset,),
                device_id_type=MESH,
            ).start()

        @pl.when(jnp.logical_not(exists(me + offset, domains)))
        def _():
            for g in range(ghosts):
                ghost[k, g] = empty
            dests[k] = jnp.full(dests.shape[1:], -1, jnp.int32)

    for k, offset in enumerate(OFFSETS):

        @pl.when(exists(me - offset, domains))
        def _():
            pltpu.make_async_copy(outbox.at[k], outbox.at[k], send_sem.at[k]).wait()
            pltpu.make_async_copy(dest_row, dest_row, dest_send.at[k]).wait()

        @pl.when(exists(me + offset, domains))
        def _():
            pltpu.make_async_copy(ghost.at[k], ghost.at[k], recv_sem.at[k]).wait()
            pltpu.make_async_copy(dests.at[k], dests.at[k], dest_recv.at[k]).wait()


def exchange_kernel(domains, sign, outbox, inbox, send_sem, recv_sem):
    me = lax.axis_index("dom")
    greet(me, domains)
    for k, offset in enumerate(OFFSETS):

        @pl.when(exists(me + sign * offset, domains))
        def _():
            pltpu.make_async_remote_copy(
                src_ref=outbox.at[k],
                dst_ref=inbox.at[k],
                send_sem=send_sem.at[k],
                recv_sem=recv_sem.at[k],
                device_id=(me + sign * offset,),
                device_id_type=MESH,
            ).start()

    for k, offset in enumerate(OFFSETS):

        @pl.when(exists(me + sign * offset, domains))
        def _():
            pltpu.make_async_copy(outbox.at[k], outbox.at[k], send_sem.at[k]).wait()

        @pl.when(exists(me - sign * offset, domains))
        def _():
            pltpu.make_async_copy(inbox.at[k], inbox.at[k], recv_sem.at[k]).wait()


def exchange(blocks, domains, sign, collective_id):
    count = len(OFFSETS)
    return pl.pallas_call(
        functools.partial(exchange_kernel, domains, sign),
        out_shape=jax.ShapeDtypeStruct(blocks.shape, blocks.dtype),
        in_specs=[VMEM],
        out_specs=VMEM,
        scratch_shapes=[
            pltpu.SemaphoreType.DMA((count,)),
            pltpu.SemaphoreType.DMA((count,)),
        ],
        compiler_params=pltpu.CompilerParams(
            collective_id=collective_id, has_side_effects=True
        ),
        name=f"exchange_{collective_id}",
    )(blocks)


def spread(source, first, count, wide, rows):
    group = TILE // 8

    def step(b, carry):
        block = source[pl.ds(b * group, group)].reshape(TILE, TILE).T
        for f in range(group):
            for n, c in enumerate(rows):
                lane = f * 8 + c
                wide[first + b * group + f, n] = jnp.broadcast_to(
                    block[:, lane : lane + 1], (TILE, TILE)
                )
        return carry

    lax.fori_loop(0, count // group, step, 0)


def density_kernel(
    pair_tiles, pair_count, send_list, own, ghost, embed, energy, slope, outbox, wide
):
    tiles, frame_ghosts = own.shape[0], ghost.shape[0]
    spread(own, 0, tiles, wide, (0, 1, 2, 3))
    spread(ghost, tiles, frame_ghosts, wide, (0, 1, 2, 3))

    def tile_step(t, carry):
        mine = own[t]
        x, y, z = [jnp.broadcast_to(mine[c : c + 1], (8, TILE)) for c in range(3)]

        def pair_step(p, sums):
            rho, pair = sums
            near = pair_tiles[t, p]
            for j in range(TILE // 8):
                rows = pl.ds(j * 8, 8)
                dx = x - wide[near, 0, rows]
                dy = y - wide[near, 1, rows]
                dz = z - wide[near, 2, rows]
                reach = jnp.maximum(1.0 - (dx * dx + dy * dy + dz * dz), 0.0)
                square = reach * reach
                rho = rho + square * reach * wide[near, 3, rows]
                pair = pair + square * square
            return rho, pair

        zero = jnp.zeros((8, TILE), jnp.float32)
        rho, pair = lax.fori_loop(0, pair_count[t], pair_step, (zero, zero))
        weight, filled = mine[3:4], mine[4:5]
        rho = jnp.sum(rho, axis=0, keepdims=True) - weight
        pair = jnp.sum(pair, axis=0, keepdims=True) - filled
        root = jnp.sqrt(1.0 + rho)
        strength = embed[pl.ds(t, 1), :]
        slope[pl.ds(t, 1), :] = -0.5 * strength * filled / root
        energy[pl.ds(t, 1), :] = filled * (-strength * root + 0.5 * REPULSE * pair)
        return carry

    lax.fori_loop(0, tiles, tile_step, 0)
    for k in range(send_list.shape[1]):
        for g in range(send_list.shape[2]):
            outbox[k, g : g + 1, :] = slope[pl.ds(send_list[0, k, g], 1), :]


def force_kernel(
    domains,
    pair_tiles,
    pair_count,
    dest,
    own,
    ghost,
    slope,
    ghost_slope,
    positions,
    velocity,
    force,
    outbox,
    stay,
    wide,
    packed,
    ranks,
):
    me = lax.axis_index("dom")
    tiles, frame_ghosts = own.shape[0], ghost.shape[0]
    spans = len(OFFSETS)
    each = frame_ghosts // spans
    packed[0:tiles] = own[...]
    packed[tiles:] = ghost[...]
    for t in range(tiles):
        packed[t, 5:6, :] = 3.0 * slope[t : t + 1, :]
    for k, offset in enumerate(OFFSETS):
        real = exists(me + offset, domains)
        for g in range(each):
            packed[tiles + k * each + g, 5:6, :] = jnp.where(
                real, 3.0 * ghost_slope[k, g : g + 1, :], 0.0
            )
    spread(packed, 0, tiles + frame_ghosts, wide, (0, 1, 2, 3, 5))
    for k in range(spans + 1):
        ranks[k] = 0

    def tile_step(t, carry):
        mine = packed[t]
        x, y, z, weight, tilt = [
            jnp.broadcast_to(mine[c : c + 1], (8, TILE)) for c in (0, 1, 2, 3, 5)
        ]

        def pair_step(p, sums):
            fx, fy, fz = sums
            near = pair_tiles[t, p]
            for j in range(TILE // 8):
                rows = pl.ds(j * 8, 8)
                dx = x - wide[near, 0, rows]
                dy = y - wide[near, 1, rows]
                dz = z - wide[near, 2, rows]
                reach = jnp.maximum(1.0 - (dx * dx + dy * dy + dz * dz), 0.0)
                mixed = tilt * wide[near, 3, rows] + weight * wide[near, 4, rows]
                coef = reach * reach * (mixed + (4.0 * REPULSE) * reach)
                fx = fx + coef * dx
                fy = fy + coef * dy
                fz = fz + coef * dz
            return fx, fy, fz

        zero = jnp.zeros((8, TILE), jnp.float32)
        sums = lax.fori_loop(0, pair_count[t], pair_step, (zero, zero, zero))
        filled = mine[4:5]
        columns = pl.ds(pl.multiple_of(t * TILE, TILE), TILE)
        pull = filled * jnp.concatenate(
            [jnp.sum(s, axis=0, keepdims=True) for s in sums], axis=0
        )
        force[:, columns] = pull
        new_vel = velocity[:, columns] + TIME_STEP * pull
        new_pos = positions[:, columns] + TIME_STEP * new_vel
        tile = jnp.concatenate([new_pos, new_vel, filled, jnp.zeros_like(filled)], axis=0)
        relative = dest[t] - me
        place = jnp.where(relative < 0, relative + RADIUS, relative + RADIUS - 1)
        place = jnp.where(relative == 0, spans, place)
        rank = ranks[place]
        ranks[place] = rank + 1

        @pl.when(relative == 0)
        def _():
            stay[rank] = tile

        @pl.when(relative != 0)
        def _():
            outbox[place, rank] = tile

        return carry

    lax.fori_loop(0, tiles, tile_step, 0)


def settle_kernel(dest, dests, inbox, stay, moved, count):
    me = lax.axis_index("dom")
    tiles, slots = dest.shape[0], moved.shape[1] // TILE
    rows = moved.shape[0]
    spans = len(OFFSETS)

    def put(e, tile, atoms):
        moved[:, pl.ds(pl.multiple_of(e * TILE, TILE), TILE)] = tile[0:rows]
        return atoms + tile

    def hits(value_of):
        total = jnp.int32(0)
        for i in range(tiles):
            total = total + (value_of(i) == me).astype(jnp.int32)
        return total

    slot = jnp.int32(0)
    atoms = jnp.zeros((8, TILE), jnp.float32)

    for k in range(spans):
        if k == RADIUS:
            here = hits(lambda i: dest[i])
            atoms = lax.fori_loop(
                0, here, lambda r, a, s=slot: put(s + r, stay[r], a), atoms
            )
            slot = slot + here
        here = hits(lambda i: dests[k, 0, i])
        atoms = lax.fori_loop(
            0, here, lambda r, a, s=slot: put(s + r, inbox[spans - 1 - k, r], a), atoms
        )
        slot = slot + here

    def clear(e, carry):
        moved[:, pl.ds(pl.multiple_of(e * TILE, TILE), TILE)] = jnp.zeros(
            (rows, TILE), jnp.float32
        )
        return carry

    lax.fori_loop(slot, slots, clear, 0)
    count[0] = jnp.sum(atoms[6:7]).astype(jnp.int32)


def per_device(
    positions,
    velocity,
    density_weight,
    embed_strength,
    occupied,
    send_list,
    send_count,
    pair_tiles,
    pair_count,
    migrate_dest,
):
    tiles = pair_tiles.shape[0]
    spans, ghosts = send_list.shape[1:]
    domains = lax.axis_size("dom")
    capacity = tiles + 2 * RADIUS * MMAX
    f32, i32 = jnp.float32, jnp.int32

    def rows_of(flat):
        return flat.reshape(tiles, TILE)

    own, ghost, dests = pl.pallas_call(
        functools.partial(frame_kernel, domains),
        out_shape=(
            jax.ShapeDtypeStruct((tiles, 8, TILE), f32),
            jax.ShapeDtypeStruct((spans, ghosts, 8, TILE), f32),
            jax.ShapeDtypeStruct((spans, 1, TILE), i32),
        ),
        in_specs=[SMEM, SMEM, VMEM, VMEM, VMEM, VMEM],
        out_specs=(VMEM, VMEM, VMEM),
        scratch_shapes=[
            pltpu.VMEM((spans, ghosts, 8, TILE), f32),
            pltpu.VMEM((1, TILE), i32),
            pltpu.SemaphoreType.DMA((spans,)),
            pltpu.SemaphoreType.DMA((spans,)),
            pltpu.SemaphoreType.DMA((spans,)),
            pltpu.SemaphoreType.DMA((spans,)),
        ],
        compiler_params=pltpu.CompilerParams(collective_id=0, has_side_effects=True),
        name="frame",
    )(
        send_list,
        send_count,
        positions,
        rows_of(density_weight),
        rows_of(occupied),
        migrate_dest.reshape(1, tiles),
    )
    ghost = ghost.reshape(spans * ghosts, 8, TILE)
    energy, slope, slope_out = pl.pallas_call(
        density_kernel,
        out_shape=(
            jax.ShapeDtypeStruct((tiles, TILE), f32),
            jax.ShapeDtypeStruct((tiles, TILE), f32),
            jax.ShapeDtypeStruct((spans, ghosts, TILE), f32),
        ),
        in_specs=[SMEM, SMEM, SMEM, VMEM, VMEM, VMEM],
        out_specs=(VMEM, VMEM, VMEM),
        scratch_shapes=[pltpu.VMEM((tiles + spans * ghosts, 4, TILE, TILE), f32)],
        compiler_params=pltpu.CompilerParams(vmem_limit_bytes=WIDE),
        name="density",
    )(pair_tiles, pair_count, send_list, own, ghost, rows_of(embed_strength))
    ghost_slope = exchange(slope_out, domains, -1, 1)
    force, outbox, stay = pl.pallas_call(
        functools.partial(force_kernel, domains),
        out_shape=(
            jax.ShapeDtypeStruct(positions.shape, f32),
            jax.ShapeDtypeStruct((spans, MMAX, 8, TILE), f32),
            jax.ShapeDtypeStruct((tiles, 8, TILE), f32),
        ),
        in_specs=[SMEM, SMEM, SMEM] + [VMEM] * 6,
        out_specs=(VMEM, VMEM, VMEM),
        scratch_shapes=[
            pltpu.VMEM((tiles + spans * ghosts, 5, TILE, TILE), f32),
            pltpu.VMEM((tiles + spans * ghosts, 8, TILE), f32),
            pltpu.SMEM((spans + 1,), i32),
        ],
        compiler_params=pltpu.CompilerParams(vmem_limit_bytes=WIDE),
        name="force",
    )(
        pair_tiles,
        pair_count,
        migrate_dest,
        own,
        ghost,
        slope,
        ghost_slope,
        positions,
        velocity,
    )
    inbox = exchange(outbox, domains, 1, 2)
    moved, moved_count = pl.pallas_call(
        settle_kernel,
        out_shape=(
            jax.ShapeDtypeStruct((7, capacity * TILE), f32),
            jax.ShapeDtypeStruct((1,), i32),
        ),
        in_specs=[SMEM, SMEM, VMEM, VMEM],
        out_specs=(VMEM, SMEM),
        name="settle",
    )(migrate_dest, dests, inbox, stay)
    return (force, energy.reshape(tiles * TILE), moved, moved_count)


def solution(mesh):
    placed = (
        P(None, "dom"),
        P(None, "dom"),
        P("dom"),
        P("dom"),
        P("dom"),
        P("dom", None, None),
        P("dom", None),
        P("dom", None),
        P("dom"),
        P("dom"),
    )
    return jax.shard_map(
        per_device,
        mesh=mesh,
        in_specs=placed,
        out_specs=(P(None, "dom"), P("dom"), P(None, "dom"), P("dom")),
        check_vma=False,
    )
```

time: 434 us -> 104 us (0.24)
  starting transfers between devices: 132 us -> 0 us
  other arithmetic: 121 us -> 0 us
  Pallas kernels: 0 us -> 101 us
  matrix products: 82.1 us -> 0 us
  blocking collectives: 36.3 us -> 0 us
  waiting for transfers between devices: 27.8 us -> 0 us
  local copies, waits for them, and re-layouts: 25.8 us -> 1.38 us
    ppermute x40 -> x0, starting transfers between devices: 132 us -> none  [shifted(): return lax.ppermute(block, axis, route)]
    pallas_call x0 -> x6, Pallas kernels: none -> 101 us  [the longest x1 39.6 us: per_device(): pl.pallas_call(functools.partial(force_kernel, domains), out_shape=(jax.S...]
    reduce_sum x10 -> x0, other arithmetic: 98.2 us -> none  [the longest x4 52.8 us: force_terms(): total_coef = jnp.sum(pair_coef, axis=(1, 3))]
    dot_general x4 -> x0, matrix products: 82.1 us -> none  [force_terms(): jnp.einsum('bpij,bpcj->bci', pair_coef, near_pos, precision=EXACT_PRODUCT)]
    unnamed x1 -> x0, blocking collectives: 36.3 us -> none
    ppermute x40 -> x0, waiting for transfers between devices: 27.8 us -> none  [shifted(): return lax.ppermute(block, axis, route)]
    select_n x50 -> x0, other arithmetic: 16.5 us -> none  [the longest x8 14.1 us: per_device(): moved_tiles = moved_tiles.at[slot_list].set(arrived, mode='drop')]
    gather x14 -> x0, local copies, waits for them, and re-layouts: 11.2 us -> none  [the longest x4 3.59 us: density_block(): nearby = frame_tiles[slot_list]]
  transfers between devices with their start and end apart: 40 -> 0, of which waited for: 11 -> 0; matrix products, arithmetic and copies ran while one was open for 52% -> 0% of each run, Pallas kernels for 0% -> 0%
where the time goes in v1:
time: 104 us; the launch traced here: 103 us
  Pallas kernels  101 us (97%)
  local copies, waits for them, and re-layouts  1.38 us (1%)
    pallas_call x1, Pallas kernels, per_device(): pl.pallas_call(functools.partial(force_kernel, domains), out_shape=(jax.S...  39.6 us
    pallas_call x1, Pallas kernels, per_device(): pl.pallas_call(density_kernel, out_shape=(jax.ShapeDtypeStruct((tiles, TI...  30.9 us
    pallas_call x2, Pallas kernels, exchange(): pl.pallas_call(functools.partial(exchange_kernel, domains, sign), out_sha...  18.6 us
    pallas_call x1, Pallas kernels, per_device(): pl.pallas_call(functools.partial(frame_kernel, domains), out_shape=(jax.S...  9.22 us
    pallas_call x1, Pallas kernels, per_device(): pl.pallas_call(settle_kernel, out_shape=(jax.ShapeDtypeStruct((7, capacit...  2.44 us

profile of v1, /device:TPU:17, one launch (start us, length us, event | category | flops | bytes accessed | tf_op | source)
XLA Modules:
  0.0 102.8 jit_solution(13322326048284880279)
XLA Ops:
  0.6 1.4 %copy.15.pair_tiles = s32[32,24]{1,0:T(8,128)} copy(s32[32,24]{0,1:T(8,128)} %param.17) | data formatting | bytes 6144 | tf_op args[7]
  2.0 9.2 %frame.1 = (f32[32,8,128]{2,1,0:T(8,128)}, f32[8,8,8,128]{3,2,1,0:T(8,128)}, s32[8,1,128]{2,1,0:T(1,128)}) custom-call(s32[1,8,8]{2,1,0:T(8,128)} %send_list.3, s32[1,8]{1,0:T(1,128)} %send_count.1, f32[3,4096]{1,0:T(4,128)} %positions.3, f32[32,128]{1,0:T(8,128)} %bitcast.8, s32[32,128]{1,0:T(8,128)} %bitcast.9, s32[1,32]{1,0:T(1,128)} %bitcast.11), custom_call_target="tpu_custom_call" | custom-call | tf_op jit(solution)/shard_map/frame/pallas_call | solution.py:379
  11.2 30.9 %density.1 = (f32[32,128]{1,0:T(8,128)}, f32[32,128]{1,0:T(8,128)}, f32[8,8,128]{2,1,0:T(8,128)}) custom-call(s32[32,24]{1,0:T(8,128)} %copy.15.pair_tiles, s32[32]{0:T(128)} %pair_count.3, s32[1,8,8]{2,1,0:T(8,128)} %send_list.3, f32[32,8,128]{2,1,0:T(8,128)} %get-tuple-element.15.own, f32[64,8,128]{2,1,0:T(8,128)} %bitcast.6, f32[32,128]{1,0:T(8,128)} %bitcast.10), custom_call_target="tpu_custom_call" | custom-call | tf_op jit(solution)/shard_map/density/pallas_call | solution.py:407
  42.1 9.2 %exchange_1.1.ghost_slope = f32[8,8,128]{2,1,0:T(8,128)} custom-call(f32[8,8,128]{2,1,0:T(8,128)} %get-tuple-element.18.outbox), custom_call_target="tpu_custom_call" | custom-call | tf_op jit(solution)/shard_map/exchange_1/pallas_call | solution.py:154
  51.4 39.6 %force.1 = (f32[3,4096]{1,0:T(4,128)}, f32[8,4,8,128]{3,2,1,0:T(8,128)}, f32[32,8,128]{2,1,0:T(8,128)}) custom-call(s32[32,24]{1,0:T(8,128)} %copy.15.pair_tiles, s32[32]{0:T(128)} %pair_count.3, s32[32]{0:T(128)} %dest.3, f32[32,8,128]{2,1,0:T(8,128)} %get-tuple-element.15.own, f32[64,8,128]{2,1,0:T(8,128)} %bitcast.7, f32[32,128]{1,0:T(8,128)} %get-tuple-element.17.slope, ...), custom_call_target="tpu_custom_call" | custom-call | tf_op jit(solution)/shard_map/force/pallas_call | solution.py:421
  91.0 9.3 %exchange_2.1.inbox = f32[8,4,8,128]{3,2,1,0:T(8,128)} custom-call(f32[8,4,8,128]{3,2,1,0:T(8,128)} %get-tuple-element.22.outbox), custom_call_target="tpu_custom_call" | custom-call | tf_op jit(solution)/shard_map/exchange_2/pallas_call | solution.py:154
  100.3 2.4 %settle.1 = (f32[7,8192]{1,0:T(8,128)}, s32[1]{0:T(128)}) custom-call(s32[32]{0:T(128)} %dest.3, s32[8,1,128]{2,1,0:T(1,128)} %get-tuple-element.21.dests, f32[8,4,8,128]{3,2,1,0:T(8,128)} %exchange_2.1.inbox, f32[32,8,128]{2,1,0:T(8,128)} %get-tuple-element.23.stay), custom_call_target="tpu_custom_call" | custom-call | tf_op jit(solution)/shard_map/settle/pallas_call | solution.py:449
